TPU v7x, 32 devices: a whole 2x2x4 slice. The times are simulated.
32 devices in a mesh: grp: 2 (over x), wide: 16 (over z, y, core).
Axes of the slice: x: 2, y: 2, z: 4, core: 2. Of those that a mesh axis runs over, the one named last changes fastest.
Arguments:
- hidden: bfloat16 [32, 256, 8192], P(('grp', 'wide')), parts along dimension 0, may hold values from -6 to 6
- output_gradient: bfloat16 [32, 256, 8192], P(('grp', 'wide')), parts along dimension 0, may hold values from -6 to 6
- adapter_up_factor: bfloat16 [8192, 64], replicated, may hold values from -0.0625 to 0.0625
- first_moment_estimate: float32 [64, 8192], P(None, 'wide'), may hold values from -0.06 to 0.06
- second_moment_estimate: float32 [64, 8192], P(None, 'wide'), may hold values from 0.0001 to 0.01
- lengths: int32 [32], P(('grp', 'wide')), parts along dimension 0, may hold values from 32 to 256, as said below
- seeds: int32 [128], P('wide'), may hold values from 0 to 16777215
Outputs:
- features: float32 [32, 4096], P(('grp', 'wide')), parts along dimension 0
There are 2 independent parts, one for each index of `grp`. A program takes and returns all parts, laid end to end along the dimension named above; an argument that names none is the same for every part. Nothing has to cross between parts.
Inputs may be any that keep to these rules, and one draw needn't show every extreme that they name: `lengths`: some sequence has exactly 256 live tokens and some has 32.
All inputs are finite; a program needn't handle non-finite values.
Results may differ from a plain program's by a relative error of at most 0.0039.
Values may be sent and summed in bfloat16 or wider, within the bound.
No kernel may reach another device: no remote copies, remote signals or barrier semaphores. Data moves between devices by JAX's collectives and lax.ppermute only.
A program may use at most 384 MiB of HBM per device.

v0:
```python
import jax
import jax.numpy as jnp
from jax import lax
from jax.sharding import PartitionSpec as P

K = 4096
CB = 64
RB = 8


def mix_bits(hashed):
    for turn in range(2):
        hashed = hashed & 2147483647
        hashed = hashed ^ jnp.right_shift(hashed, 16)
        hashed = hashed * 73244475
    hashed = hashed & 2147483647
    hashed = hashed ^ jnp.right_shift(hashed, 16)
    return hashed


def build_signs(rank_rows, own_cols, seeds):
    col_blocks = own_cols // CB
    row_groups = rank_rows // RB
    row_ids = lax.broadcasted_iota(jnp.int32, (RB, CB, K), 0)
    col_ids = lax.broadcasted_iota(jnp.int32, (RB, CB, K), 1)
    feat_ids = lax.broadcasted_iota(jnp.int32, (RB, CB, K), 2)

    def fill_step(loop_index, table):
        loop_index = loop_index.astype(jnp.int32)
        col_pos = loop_index // row_groups
        grp_pos = loop_index % row_groups
        param_ids = (grp_pos * RB + row_ids) * CB + col_ids
        hashed = mix_bits(param_ids * 1000003 + feat_ids * 7919 + seeds[col_pos])
        block = (1 - 2 * (hashed & 1)).astype(jnp.bfloat16)
        return lax.dynamic_update_slice(table, block, (grp_pos * RB, col_pos * CB, jnp.int32(0)))

    table = jnp.zeros((rank_rows, own_cols, K), jnp.bfloat16)
    table = lax.fori_loop(0, col_blocks * row_groups, fill_step, table)
    return table.reshape(rank_rows * own_cols, K)


def shards(
    hidden,
    output_gradient,
    adapter_up_factor,
    first_moment_estimate,
    second_moment_estimate,
    lengths,
    seeds,
):
    own_seqs, tok_slots = (hidden.shape[0], hidden.shape[1])
    rank_reduced = jnp.einsum(
        "nuk,kv->nuv", output_gradient, adapter_up_factor, preferred_element_type=jnp.float32
    )
    live_mask = lax.broadcasted_iota(jnp.int32, (own_seqs, tok_slots), 1) < lengths[:, None]
    rank_reduced = jnp.where(live_mask[:, :, None], rank_reduced, 0.0).astype(jnp.bfloat16)
    summed = jnp.einsum("str,std->srd", rank_reduced, hidden, preferred_element_type=jnp.float32)
    seq_grad = (summed / lengths.astype(jnp.float32)[:, None, None]).astype(jnp.bfloat16)
    regrouped = lax.all_to_all(seq_grad, "wide", split_axis=2, concat_axis=0, tiled=True)
    grad_full = regrouped.astype(jnp.float32)
    first_new = 0.9 * first_moment_estimate[None] + 0.1 * grad_full
    second_new = 0.999 * second_moment_estimate[None] + 0.001 * grad_full * grad_full
    update = (first_new / (jnp.sqrt(second_new) + 1e-08)).astype(jnp.bfloat16)
    all_seqs, rank_rows, own_cols = update.shape
    flat_update = update.reshape(all_seqs, rank_rows * own_cols)
    signs = build_signs(rank_rows, own_cols, seeds)
    partial_value = jnp.dot(flat_update, signs, preferred_element_type=jnp.float32)
    totals = lax.psum(partial_value, "wide")
    own_rows = lax.dynamic_slice_in_dim(totals, lax.axis_index("wide") * own_seqs, own_seqs, 0)
    return own_rows * lax.rsqrt(jnp.mean(own_rows * own_rows, axis=1, keepdims=True) + 1e-06)


def solution(mesh):
    placed = (
        P(("grp", "wide"), None, None),
        P(("grp", "wide"), None, None),
        P(),
        P(None, "wide"),
        P(None, "wide"),
        P(("grp", "wide")),
        P("wide"),
    )
    return jax.shard_map(
        shards, mesh=mesh, in_specs=placed, out_specs=P(("grp", "wide"), None), check_vma=False
    )
```

profile of v0, /device:TPU:0, one launch (start us, length us, event | category | flops | bytes accessed | tf_op | source)
XLA Modules:
  0.0 859.6 jit_solution(11713822607061688417)
XLA Ops:
  21.7 45.2 %reduce.1 = bf16[8192,64]{1,0:T(8,128)(2,1)S(1)} reduce(bf16[8192,1,64]{2,1,0:T(2,128)(2,1)} %bitcast.44, bf16[]{:T(256)} %broadcast.116), dimensions={1}, to_apply=%bitcast.32.reduce_sub_computation | reduce | bytes 2097154
  69.1 7.4 all-to-all-start
  76.8 81.1 %broadcast_in_dim.23 = bf16[64,512,4096]{2,1,0:T(8,128)(2,1)} broadcast(bf16[]{:T(256)} %constant.173.clone.1), dimensions={} | broadcast | bytes 268435456 | tf_op jit(solution)/shard_map/broadcast_in_dim | solution.py:37
  157.9 496.9 %while.16 = (s32[]{:T(128)}, bf16[64,512,4096]{2,1,0:T(8,128)(2,1)}, s32[8]{0:T(128)S(1)}, s32[]{:T(128)}, s32[]{:T(128)}, /*index=5*/s32[]{:T(128)}, s32[]{:T(1...) while((s32[]{:T(128)}, bf16[64,512,4096]{2,1,0:T(8,128)(2,1)}, s32[8]{0:T(128)S(1)}, ...), condition=%wide.region_1.2_spmd.clone, body=%wide.region_0.1_spmd.clone.sunk | while | flops 46137368 | bytes 4195198 | solution.py:38
  158.5 7.2 fusion.57
  166.3 7.2 fusion.57
  174.1 7.2 fusion.57
  181.9 7.2 fusion.57
  189.7 7.2 fusion.57
  205.2 7.2 fusion.57
  213.0 7.2 fusion.57
  220.8 7.2 fusion.57
  236.3 7.2 fusion.57
  251.8 7.2 fusion.57
  267.4 7.2 fusion.57
  290.7 7.2 fusion.57
  321.7 7.2 fusion.57
  329.4 7.2 fusion.57
  337.2 7.2 fusion.57
  352.7 7.2 fusion.57
  383.7 7.2 fusion.57
  399.2 7.2 fusion.57
  406.9 7.2 fusion.57
  414.7 7.2 fusion.57
  422.5 7.2 fusion.57
  430.2 7.2 fusion.57
  438.0 7.2 fusion.57
  445.8 7.2 fusion.57
  453.6 7.2 fusion.57
  461.3 7.2 fusion.57
  469.1 7.2 fusion.57
  476.9 7.2 fusion.57
  484.6 7.2 fusion.57
  500.1 7.2 fusion.57
  507.9 7.2 fusion.57
  515.7 7.2 fusion.57
  523.5 7.2 fusion.57
  569.9 7.2 fusion.57
  585.4 7.2 fusion.57
  593.2 7.2 fusion.57
  601.0 7.2 fusion.57
  608.7 7.2 fusion.57
  624.2 7.2 fusion.57
  632.0 7.2 fusion.57
  639.8 7.2 fusion.57
  661.8 8.5 bitcast_convert_fusion
  673.6 84.2 %convolution_bitcast_fusion = f32[16,4096]{1,0:T(8,128)} fusion(bf16[64,512,4096]{2,1,0:T(8,128)(2,1)} %get-tuple-element.162, f32[1,64,16,512]{3,2,1,0:T(8,128)S(1)} %copy.9, f32[64,512]{1,0:T(8,128)S(1)} %get-tuple-element.179, f32[64,512]{1,0:T(8,128)S(1)} %get-tuple-element.180), kind=kOutput, calls=%fused_computation.26 | convolution fusion | flops 4299161600 | bytes 271056896 | tf_op jit(solution)/shard_map/dot_general | solution.py:67
  757.8 91.2 %all-reduce.2.cloned.1.call-done = f32[16,4096]{1,0:T(8,128)} async-done(((f32[16,4096]{1,0:T(8,128)}), f32[16,4096]{1,0:T(8,128)}) %all-reduce.2.cloned.1.call-update) | async-done | bytes 262160 | tf_op jit(solution)/shard_map/psum | solution.py:68
  (108 shorter events, 232.9 us)
Async XLA Ops:
  6.5 1.2 copy-start
  69.1 585.7 %all-to-all-start = ((bf16[16,2,16384]{2,1,0:T(2,128)(2,1)}), bf16[16,2,16384]{2,1,0:T(2,128)(2,1)S(1)}, u32[]{:S(2)}, u32[]{:S(2)}) async-start(bf16[16,2,16384]{2,1,0:T(2,128)(2,1)} %reshape.53), calls=%async_computation | async-start | bytes 2097152 | tf_op jit(solution)/shard_map/all_to_all | solution.py:59
  76.5 772.5 %all-reduce.2.cloned.1.call-start = ((), (), s32[]{:S(2)}) async-start(), calls=%async_computation.1 | async-start | bytes 524288 | tf_op jit(solution)/shard_map/psum | solution.py:68
  76.8 81.1 %copy-start.3 = (s32[8]{0:T(128)S(1)}, s32[8]{0:T(128)}, u32[]{:S(2)}) copy-start(s32[8]{0:T(128)} %param.15) | copy-start | bytes 100
  157.9 496.9 %copy-start.1 = (f32[64,512]{1,0:T(8,128)S(1)}, f32[64,512]{1,0:T(8,128)}, u32[]{:S(2)}) copy-start(f32[64,512]{1,0:T(8,128)} %param.13) | copy-start | bytes 393220
  157.9 496.9 %copy-start.2 = (f32[64,512]{1,0:T(8,128)S(1)}, f32[64,512]{1,0:T(8,128)}, u32[]{:S(2)}) copy-start(f32[64,512]{1,0:T(8,128)} %param.12) | copy-start | bytes 393220
Sparse Core Ops, SparseCore 0:
  758.0 91.0 all-reduce.1
where the time goes:
time: 861 us; the launch traced here: 860 us
  other arithmetic  515 us (60%)
  local copies, waits for them, and re-layouts  140 us (16%)
  waiting for transfers between devices  91.2 us (11%)
  matrix products  90.7 us (11%)
  between operations  14.9 us (2%)
    dynamic_update_slice x64, other arithmetic, fill_step(): lax.dynamic_update_slice(table, block, (grp_pos * RB, col_pos * CB, jnp.i...  459 us
    psum x1, waiting for transfers between devices, shards(): totals = lax.psum(partial_value, 'wide')  91.2 us
    dot_general x1, matrix products, shards(): jnp.dot(flat_update, signs, preferred_element_type=jnp.float32)  84.2 us
    broadcast_in_dim x1, local copies, waits for them, and re-layouts, build_signs(): table = jnp.zeros((rank_rows, own_cols, K), jnp.bfloat16)  81.1 us
    unnamed x1, other arithmetic  45.2 us
    dynamic_slice x64, local copies, waits for them, and re-layouts, fill_step(): hashed = mix_bits(param_ids * 1000003 + feat_ids * 7919 + seeds[col_pos])  38.1 us
  transfers between devices with their start and end apart: 2, of which 1 were waited for; matrix products, arithmetic and copies ran while one was open for 67% of the time, Pallas kernels for 0%

commit v1 on v0

--- a/solution.py
+++ b/solution.py
@@ -65,7 +65,9 @@
     flat_update = update.reshape(all_seqs, rank_rows * own_cols)
     signs = build_signs(rank_rows, own_cols, seeds)
     partial_value = jnp.dot(flat_update, signs, preferred_element_type=jnp.float32)
-    totals = lax.psum(partial_value, "wide")
+    totals = partial_value
+    for hop in (1, 2, 4, 8):
+        totals = totals + lax.ppermute(totals, "wide", [(dev, dev ^ hop) for dev in range(16)])
     own_rows = lax.dynamic_slice_in_dim(totals, lax.axis_index("wide") * own_seqs, own_seqs, 0)
     return own_rows * lax.rsqrt(jnp.mean(own_rows * own_rows, axis=1, keepdims=True) + 1e-06)
 

time: 861 us -> 788 us (0.915)
  waiting for transfers between devices: 91.2 us -> 25.2 us
  between operations: 14.9 us -> 1.52 us
    psum x1 -> x0, waiting for transfers between devices: 91.2 us -> none  [shards(): totals = lax.psum(partial_value, 'wide')]
    ppermute x0 -> x4, waiting for transfers between devices: none -> 25.2 us  [shards(): lax.ppermute(totals, 'wide', [(dev, dev ^ hop) for dev in range(16)])]
  transfers between devices with their start and end apart: 2 -> 5, of which waited for: 1 -> 4; matrix products, arithmetic and copies ran while one was open for 67% -> 74% of each run, Pallas kernels for 0% -> 0%
where the time goes in v1:
time: 788 us; the launch traced here: 787 us
  other arithmetic  515 us (65%)
  local copies, waits for them, and re-layouts  140 us (18%)
  matrix products  90.7 us (12%)
  waiting for transfers between devices  25.2 us (3%)
  starting transfers between devices  13.9 us (2%)
    dynamic_update_slice x64, other arithmetic, fill_step(): lax.dynamic_update_slice(table, block, (grp_pos * RB, col_pos * CB, jnp.i...  459 us
    dot_general x1, matrix products, shards(): jnp.dot(flat_update, signs, preferred_element_type=jnp.float32)  84.2 us
    broadcast_in_dim x1, local copies, waits for them, and re-layouts, build_signs(): table = jnp.zeros((rank_rows, own_cols, K), jnp.bfloat16)  81.1 us
    unnamed x1, other arithmetic  45.2 us
    dynamic_slice x64, local copies, waits for them, and re-layouts, fill_step(): hashed = mix_bits(param_ids * 1000003 + feat_ids * 7919 + seeds[col_pos])  38.7 us
    ppermute x4, waiting for transfers between devices, shards(): lax.ppermute(totals, 'wide', [(dev, dev ^ hop) for dev in range(16)])  25.2 us
  transfers between devices with their start and end apart: 5, of which 4 were waited for; matrix products, arithmetic and copies ran while one was open for 74% of the time, Pallas kernels for 0%

profile of v1, /device:TPU:0, one launch (start us, length us, event | category | flops | bytes accessed | tf_op | source)
XLA Modules:
  0.0 786.6 jit_solution(4560282126885838998)
XLA Ops:
  15.1 45.2 %reduce.1 = bf16[8192,64]{1,0:T(8,128)(2,1)S(1)} reduce(bf16[8192,1,64]{2,1,0:T(2,128)(2,1)} %bitcast.44, bf16[]{:T(256)} %broadcast.116), dimensions={1}, to_apply=%bitcast.32.reduce_sub_computation | reduce | bytes 2097154
  62.6 7.4 all-to-all-start
  70.0 81.1 %broadcast_in_dim.23 = bf16[64,512,4096]{2,1,0:T(8,128)(2,1)} broadcast(bf16[]{:T(256)} %constant.173.clone.1), dimensions={} | broadcast | bytes 268435456 | tf_op jit(solution)/shard_map/broadcast_in_dim | solution.py:37
  151.1 497.8 %while.16 = (s32[]{:T(128)}, bf16[64,512,4096]{2,1,0:T(8,128)(2,1)}, s32[8]{0:T(128)S(1)}, s32[]{:T(128)}, s32[]{:T(128)}, /*index=5*/s32[]{:T(128)}, s32[]{:T(1...) while((s32[]{:T(128)}, bf16[64,512,4096]{2,1,0:T(8,128)(2,1)}, s32[8]{0:T(128)S(1)}, ...), condition=%wide.region_1.2_spmd.clone, body=%wide.region_0.1_spmd.clone.sunk | while | flops 46137368 | bytes 4195198 | solution.py:38
  151.8 7.2 fusion.57
  167.3 7.2 fusion.57
  175.1 7.2 fusion.57
  182.9 7.2 fusion.57
  198.5 7.2 fusion.57
  206.3 7.2 fusion.57
  214.0 7.2 fusion.57
  221.8 7.2 fusion.57
  229.6 7.2 fusion.57
  237.4 7.2 fusion.57
  245.2 7.2 fusion.57
  253.0 7.2 fusion.57
  260.8 7.2 fusion.57
  268.5 7.2 fusion.57
  284.1 7.2 fusion.57
  299.6 7.2 fusion.57
  315.2 7.2 fusion.57
  361.8 7.2 fusion.57
  392.9 7.2 fusion.57
  400.7 7.2 fusion.57
  408.4 7.2 fusion.57
  416.2 7.2 fusion.57
  431.8 7.2 fusion.57
  439.5 7.2 fusion.57
  447.3 7.2 fusion.57
  470.7 7.2 fusion.57
  478.4 7.2 fusion.57
  486.2 7.2 fusion.57
  494.0 7.2 fusion.57
  501.8 7.2 fusion.57
  509.6 7.2 fusion.57
  517.3 7.2 fusion.57
  532.9 7.2 fusion.57
  563.9 7.2 fusion.57
  587.2 7.2 fusion.57
  595.0 7.2 fusion.57
  602.8 7.2 fusion.57
  610.6 7.2 fusion.57
  618.3 7.2 fusion.57
  626.1 7.2 fusion.57
  633.9 7.2 fusion.57
  655.9 8.5 %bitcast_convert_fusion = f32[1,64,8192]{1,0,2:T(1,128)} fusion(bf16[8192,1,64]{2,1,0:T(2,128)(2,1)} %reshape.54), kind=kLoop, calls=%fused_computation.57 | loop fusion | flops 524288 | bytes 3145728 | tf_op jit(solution)/shard_map/convert_element_type | solution.py:60
  667.7 84.2 %convolution_bitcast_fusion = f32[16,4096]{1,0:T(8,128)} fusion(bf16[64,512,4096]{2,1,0:T(8,128)(2,1)} %get-tuple-element.162, f32[1,64,16,512]{3,2,1,0:T(8,128)S(1)} %copy.9, f32[64,512]{1,0:T(8,128)S(1)} %get-tuple-element.181, f32[64,512]{1,0:T(8,128)S(1)} %get-tuple-element.182), kind=kOutput, calls=%fused_computation.26 | convolution fusion | flops 4299161600 | bytes 271056896 | tf_op jit(solution)/shard_map/dot_general | solution.py:67
  773.5 11.1 %collective-permute-done.3 = f32[16,4096]{1,0:T(8,128)S(1)} collective-permute-done((f32[16,4096]{1,0:T(8,128)S(1)}, f32[16,4096]{1,0:T(8,128)S(1)}, u32[]{:S(2)}, u32[]{:S(2)}) %collective-permute-start.3) | collective-permute-done | bytes 262176 | tf_op jit(solution)/shard_map/ppermute | solution.py:70
  (116 shorter events, 253.1 us)
Async XLA Ops:
  0.0 1.2 copy-start
  62.6 586.4 %all-to-all-start = ((bf16[16,2,16384]{2,1,0:T(2,128)(2,1)}), bf16[16,2,16384]{2,1,0:T(2,128)(2,1)S(1)}, u32[]{:S(2)}, u32[]{:S(2)}) async-start(bf16[16,2,16384]{2,1,0:T(2,128)(2,1)} %reshape.53), calls=%async_computation | async-start | bytes 2097152 | tf_op jit(solution)/shard_map/all_to_all | solution.py:59
  70.0 81.1 %copy-start.3 = (s32[8]{0:T(128)S(1)}, s32[8]{0:T(128)}, u32[]{:S(2)}) copy-start(s32[8]{0:T(128)} %param.15) | copy-start | bytes 100
  151.1 497.8 %copy-start.1 = (f32[64,512]{1,0:T(8,128)S(1)}, f32[64,512]{1,0:T(8,128)}, u32[]{:S(2)}) copy-start(f32[64,512]{1,0:T(8,128)} %param.13) | copy-start | bytes 393220
  151.1 497.8 %copy-start.2 = (f32[64,512]{1,0:T(8,128)S(1)}, f32[64,512]{1,0:T(8,128)}, u32[]{:S(2)}) copy-start(f32[64,512]{1,0:T(8,128)} %param.12) | copy-start | bytes 393220
  751.9 1.8 collective-permute-start
  754.7 8.6 %collective-permute-start.1 = (f32[16,4096]{1,0:T(8,128)S(1)}, f32[16,4096]{1,0:T(8,128)S(1)}, u32[]{:S(2)}, u32[]{:S(2)}) collective-permute-start(f32[16,4096]{1,0:T(8,128)S(1)} %add.174), channel_id=1, source_target_pairs={{0,2},{1,3},{2,0},{3,1},{4,6},{5,7},{6,4},{7,5},{8,10},{9,11},{10,... | collective-permute-start | bytes 786440 | tf_op jit(solution)/shard_map/ppermute | solution.py:70
  763.3 7.8 collective-permute-start.2
  771.2 13.5 %collective-permute-start.3 = (f32[16,4096]{1,0:T(8,128)S(1)}, f32[16,4096]{1,0:T(8,128)S(1)}, u32[]{:S(2)}, u32[]{:S(2)}) collective-permute-start(f32[16,4096]{1,0:T(8,128)S(1)} %add.176), channel_id=1, source_target_pairs={{0,8},{1,9},{2,10},{3,11},{4,12},{5,13},{6,14},{7,15},{8,0},{9,1},... | collective-permute-start | bytes 786440 | tf_op jit(solution)/shard_map/ppermute | solution.py:70
